TPU v7x, 128 devices: a whole 4x4x4 slice. The times are simulated.
128 devices in a mesh: seq: 8 (over z, y_hi), chan: 8 (over x, core), dp: 2 (over y_lo).
Axes of the slice: x: 4, y: 4 (y_hi: 2, y_lo: 2; y = y_hi * 2 + y_lo), z: 4, core: 2. Of those that a mesh axis runs over, the one named last changes fastest.
Arguments:
- tokens: bfloat16 [2, 1024, 8192], P('dp', 'seq'), may hold values from -6 to 6
- in_weight: bfloat16 [8192, 3, 4096], P('seq', None, 'chan'), may hold values from -0.0625 to 0.0625
- short_taps: float32 [3, 3, 4096], P(None, None, 'chan'), may hold values from -1 to 1
- long_filter: float32 [1024, 4096], P('seq', 'chan'), may hold values from -1.25 to 1.25
- skip_gain: float32 [4096], P('chan'), may hold values from 0.5 to 1.5
- cotangent: bfloat16 [2, 1024, 4096], P('dp', 'seq', 'chan'), may hold values from -6 to 6
Outputs:
- hyena_out: bfloat16 [2, 1024, 4096], P('dp', 'seq', 'chan')
- grad_tokens: bfloat16 [2, 1024, 8192], P('dp', None, ('seq', 'chan'))
- grad_weight: bfloat16 [8192, 3, 4096], P('seq', None, 'chan')
- grad_filter: float32 [1024, 4096], P('seq', 'chan')
All inputs are finite; a program needn't handle non-finite values.
Results may differ from a plain program's by a relative error of at most 0.02.
Values may be sent and summed in bfloat16 or wider, within the bound.
No kernel may reach another device: no remote copies, remote signals or barrier semaphores. Data moves between devices by JAX's collectives and lax.ppermute only.
A program may use at most 128 MiB of HBM per device.

v0:
```python
import math
import jax
import jax.numpy as jnp
from jax import lax
from jax.sharding import PartitionSpec as P


def partner_2(shard, axis, stride):
    return lax.ppermute(shard, axis, [(i, i ^ 1 << stride) for i in range(lax.axis_size(axis))])


def shifted(value, axis, steps):
    count = lax.axis_size(axis)
    leading, last = (max(0, -steps), min(count, count - steps))
    return lax.ppermute(value, axis, [(source, source + steps) for source in range(leading, last)])


def complex_mul(left, right):
    return jnp.stack(
        [left[0] * right[0] - left[1] * right[1], left[0] * right[1] + left[1] * right[0]]
    )


def conjugate(signal):
    return jnp.stack([signal[0], -signal[1]])


def dft_tables(length):
    index = jnp.arange(length, dtype=jnp.int32)
    product = index[:, None] * index[None, :] % length
    phases = 2.0 * math.pi / length * product.astype(jnp.float32)
    return (jnp.cos(phases), jnp.sin(phases))


def table_apply(cos_table, sin_table, sign, signal, form):
    high = lax.Precision.HIGHEST
    real_cos = jnp.einsum(form, cos_table, signal[0], precision=high)
    imag_cos = jnp.einsum(form, cos_table, signal[1], precision=high)
    real_sin = jnp.einsum(form, sin_table, signal[0], precision=high)
    imag_sin = jnp.einsum(form, sin_table, signal[1], precision=high)
    return jnp.stack([real_cos - sign * imag_sin, imag_cos + sign * real_sin])


def reverse_bits(seq_pos, seq_count):
    bit_total = seq_count.bit_length() - 1
    result = jnp.zeros((), jnp.int32)
    for bit_pos in range(bit_total):
        result = result + seq_pos // (1 << bit_pos) % 2 * (1 << bit_total - 1 - bit_pos)
    return result


def pairs_forward(signal, seq_count, seq_pos):
    bit_total = seq_count.bit_length() - 1
    for bit_pos in reversed(range(bit_total)):
        half_span = 1 << bit_pos
        partner = partner_2(signal, "seq", bit_pos)
        offset = (seq_pos % half_span).astype(jnp.float32)
        phases = -math.pi * offset / half_span
        twiddle = jnp.stack([jnp.cos(phases), jnp.sin(phases)])
        is_upper = seq_pos // half_span % 2 == 1
        signal = jnp.where(is_upper, complex_mul(partner - signal, twiddle), signal + partner)
    return signal


def pairs_inverse(signal, seq_count, seq_pos):
    bit_total = seq_count.bit_length() - 1
    for bit_pos in range(bit_total):
        half_span = 1 << bit_pos
        partner = partner_2(signal.astype(jnp.bfloat16), "seq", bit_pos).astype(signal.dtype)
        offset = (seq_pos % half_span).astype(jnp.float32)
        phases = math.pi * offset / half_span
        twiddle = jnp.stack([jnp.cos(phases), jnp.sin(phases)])
        is_upper = seq_pos // half_span % 2 == 1
        signal = jnp.where(
            is_upper, partner - complex_mul(signal, twiddle), signal + complex_mul(partner, twiddle)
        )
    return signal


def position_twiddle(spec_order, tok_rows, full_len, sign):
    k_index = 2 * spec_order + jnp.arange(2, dtype=jnp.int32)
    pos_rows = jnp.arange(tok_rows, dtype=jnp.int32)
    product = k_index[:, None] * pos_rows[None, :] % full_len
    phases = sign * 2.0 * math.pi / full_len * product.astype(jnp.float32)
    return jnp.stack([jnp.cos(phases), jnp.sin(phases)])[:, None, :, :, None]


def forward_spectrum(rows_in, seq_count, seq_pos):
    tok_rows = rows_in.shape[1]
    full_len = 2 * seq_count * tok_rows
    phase_shift = math.pi * seq_pos.astype(jnp.float32) / seq_count
    real_part = jnp.stack([rows_in, rows_in * jnp.cos(phase_shift)], axis=1)
    imag_part = jnp.stack([jnp.zeros_like(rows_in), -rows_in * jnp.sin(phase_shift)], axis=1)
    signal = jnp.stack([real_part, imag_part])
    signal = pairs_forward(signal, seq_count, seq_pos)
    spec_order = reverse_bits(seq_pos, seq_count)
    signal = complex_mul(signal, position_twiddle(spec_order, tok_rows, full_len, -1.0))
    cos_table, sin_table = dft_tables(tok_rows)
    return table_apply(cos_table, sin_table, -1.0, signal, "ka,gbac->gbkc")


def inverse_spectrum(signal, seq_count, seq_pos):
    tok_rows = signal.shape[3]
    full_len = 2 * seq_count * tok_rows
    cos_table, sin_table = dft_tables(tok_rows)
    signal = table_apply(cos_table, sin_table, 1.0, signal, "ka,gbac->gbkc")
    spec_order = reverse_bits(seq_pos, seq_count)
    signal = complex_mul(signal, position_twiddle(spec_order, tok_rows, full_len, 1.0))
    signal = pairs_inverse(signal, seq_count, seq_pos)
    phase_shift = math.pi * seq_pos.astype(jnp.float32) / seq_count
    combined = (
        signal[0][:, 0]
        + jnp.cos(phase_shift) * signal[0][:, 1]
        - jnp.sin(phase_shift) * signal[1][:, 1]
    )
    return combined / full_len


def local(tokens, in_weight, short_taps, long_filter, skip_gain, cotangent):
    seq_count = lax.axis_size("seq")
    seq_pos = lax.axis_index("seq")
    tok_rows = tokens.shape[1]
    slab_rows = in_weight.shape[0]
    chan_cols = in_weight.shape[2]
    taps_len = short_taps.shape[1]
    grad_scale = 1.0 / math.sqrt(lax.axis_size("dp") * seq_count * tok_rows)
    spread = lax.all_to_all(tokens[0], "seq", split_axis=1, concat_axis=0, tiled=True)
    flat_weight = in_weight.reshape(slab_rows, 3 * chan_cols)
    projected = lax.psum_scatter(
        jnp.dot(spread, flat_weight, preferred_element_type=jnp.float32),
        "seq",
        scatter_dimension=0,
        tiled=True,
    ).reshape(tok_rows, 3, chan_cols)
    rim_rows = shifted(projected[tok_rows - (taps_len - 1) :], "seq", 1)
    extended = jnp.concatenate([rim_rows, projected], axis=0)
    streams = jnp.zeros_like(projected)
    for tap_pos in range(taps_len):
        begin = taps_len - 1 - tap_pos
        streams = streams + short_taps[:, tap_pos, :] * extended[begin : begin + tok_rows]
    queries = streams[:, 0]
    keys_in = streams[:, 1]
    values_in = streams[:, 2]
    gated_in = keys_in * values_in
    spectra = forward_spectrum(jnp.stack([gated_in, long_filter]), seq_count, seq_pos)
    gated_freq = spectra[:, 0:1]
    filter_freq = spectra[:, 1:2]
    conv_out = (
        inverse_spectrum(complex_mul(gated_freq, filter_freq), seq_count, seq_pos)[0]
        + skip_gain * gated_in
    )
    hyena_out = (queries * conv_out).astype(jnp.bfloat16)[None]
    grad_in = cotangent[0].astype(jnp.float32)
    d_conv = grad_in * queries
    d_query = grad_in * conv_out
    conv_freq = forward_spectrum(d_conv[None], seq_count, seq_pos)
    pair_freq = jnp.concatenate(
        [
            complex_mul(conjugate(filter_freq), conv_freq),
            complex_mul(conjugate(gated_freq), conv_freq),
        ],
        axis=1,
    )
    back_rows = inverse_spectrum(pair_freq, seq_count, seq_pos)
    d_gated = back_rows[0] + skip_gain * d_conv
    filter_part = back_rows[1] * grad_scale
    d_streams = jnp.stack([d_query, d_gated * values_in, d_gated * keys_in], axis=1)
    rim_next = shifted(d_streams[: taps_len - 1], "seq", -1)
    ext_next = jnp.concatenate([d_streams, rim_next], axis=0)
    d_projected = jnp.zeros_like(d_streams)
    for tap_pos in range(taps_len):
        d_projected = (
            d_projected + short_taps[:, tap_pos, :] * ext_next[tap_pos : tap_pos + tok_rows]
        )
    d_projected = d_projected.astype(jnp.bfloat16).reshape(tok_rows, 3 * chan_cols)
    shard_rows = lax.all_gather(d_projected, "seq", axis=0, tiled=True)
    weight_total = lax.dot_general(
        spread, shard_rows, (((0,), (0,)), ((), ())), preferred_element_type=jnp.float32
    )
    token_block = lax.dot_general(
        shard_rows, flat_weight, (((1,), (1,)), ((), ())), preferred_element_type=jnp.float32
    )
    grad_tokens = lax.psum_scatter(
        token_block.astype(jnp.bfloat16), "chan", scatter_dimension=1, tiled=True
    )[None]
    weight_sum, filter_sum = (
        lax.psum((weight_total * grad_scale).astype(jnp.bfloat16), "dp").astype(jnp.float32),
        lax.psum(filter_part.astype(jnp.bfloat16), "dp").astype(jnp.float32),
    )
    grad_weight = weight_sum.astype(jnp.bfloat16).reshape(slab_rows, 3, chan_cols)
    return (hyena_out, grad_tokens, grad_weight, filter_sum)


def solution(mesh):
    placed = (
        P("dp", "seq", None),
        P("seq", None, "chan"),
        P(None, None, "chan"),
        P("seq", "chan"),
        P("chan"),
        P("dp", "seq", "chan"),
    )
    return jax.shard_map(
        local,
        mesh=mesh,
        in_specs=placed,
        out_specs=(
            P("dp", "seq", "chan"),
            P("dp", None, ("seq", "chan")),
            P("seq", None, "chan"),
            P("seq", "chan"),
        ),
        check_vma=False,
    )
```

profile of v0, /device:TPU:0, one launch (start us, length us, event | category | flops | bytes accessed | tf_op | source)
XLA Modules:
  0.0 742.5 jit_solution(11029934226150978450)
XLA Ops:
  11.3 8.0 %all-to-all-start = ((bf16[128,8,1024]{0,2,1:T(8,128)(2,1)}), bf16[128,8,1024]{0,2,1:T(8,128)(2,1)S(1)}, u32[]{:S(2)}, u32[]{:S(2)}) async-start(bf16[128,8,1024]{0,2,1:T(8,128)(2,1)} %bitcast.318), calls=%async_computation | async-start | bytes 4194304 | tf_op jit(solution)/shard_map/all_to_all | solution.py:127
  24.0 23.8 %all-to-all-done = bf16[128,8,1024]{0,2,1:T(8,128)(2,1)S(1)} async-done(((bf16[128,8,1024]{0,2,1:T(8,128)(2,1)}), bf16[128,8,1024]{0,2,1:T(8,128)(2,1)S(1)}, u32[]{:S(2)}, u32[]{:S(2)}) %all-to-all-start) | async-done | bytes 2097184 | tf_op jit(solution)/shard_map/all_to_all | solution.py:127
  50.4 8.6 %fusion.204 = f32[1024,1536]{1,0:T(8,128)} fusion(bf16[1024,1024]{1,0:T(8,128)(2,1)} %bitcast.327, bf16[1024,1536]{0,1:T(8,128)(2,1)} %bitcast.323), kind=kOutput, calls=%fused_computation.316 | convolution fusion | flops 3221225472 | bytes 11534336 | tf_op jit(solution)/shard_map/dot_general | solution.py:130
  59.7 95.1 %reduce-scatter.5.cloned.1.call-done = f32[128,1536]{1,0:T(8,128)} async-done(((f32[1024,1536]{1,0:T(8,128)}), f32[128,1536]{1,0:T(8,128)}) %reduce-scatter.5.cloned.1.call-update) | async-done | bytes 786448 | tf_op jit(solution)/shard_map/reduce_scatter | solution.py:129
  167.7 44.0 %collective-permute-done.1 = f32[2,2,2,128,512]{4,3,1,2,0:T(8,128)} collective-permute-done((f32[2,2,2,128,512]{4,3,1,2,0:T(8,128)}, f32[2,2,2,128,512]{4,3,1,2,0:T(8,128)}, u32[]{:S(2)}, u32[]{:S(2)}) %collective-permute-start.1) | collective-permute-done | bytes 2097184 | tf_op jit(solution)/shard_map/ppermute | solution.py:9
  220.7 43.1 %collective-permute-done.2 = f32[2,2,2,128,512]{4,3,1,2,0:T(8,128)} collective-permute-done((f32[2,2,2,128,512]{4,3,1,2,0:T(8,128)}, f32[2,2,2,128,512]{4,3,1,2,0:T(8,128)}, u32[]{:S(2)}, u32[]{:S(2)}) %collective-permute-start.2) | collective-permute-done | bytes 2097184 | tf_op jit(solution)/shard_map/ppermute | solution.py:9
  269.1 4.9 maximum_select_fusion.1
  276.4 43.6 %collective-permute-done.3 = f32[2,2,2,128,512]{4,3,1,2,0:T(8,128)S(1)} collective-permute-done((f32[2,2,2,128,512]{4,3,1,2,0:T(8,128)}, f32[2,2,2,128,512]{4,3,1,2,0:T(8,128)S(1)}, u32[]{:S(2)}, u32[]{:S(2)}) %collective-permute-start.3) | collective-permute-done | bytes 2097184 | tf_op jit(solution)/shard_map/ppermute | solution.py:9
  339.2 8.7 %collective-permute-done.4 = bf16[2,1,2,128,512]{4,3,2,1,0:T(8,128)(2,1)S(1)} collective-permute-done((bf16[2,1,2,128,512]{4,3,2,1,0:T(8,128)(2,1)S(1)}, bf16[2,1,2,128,512]{4,3,2,1,0:T(8,128)(2,1)S(1)}, u32[]{:S(2)}, u32[]{:S(2)}) %collective-permute-start.4) | collective-permute-done | bytes 524320 | tf_op jit(solution)/shard_map/ppermute | solution.py:9
  350.7 8.8 %collective-permute-done.5 = bf16[2,1,2,128,512]{4,3,2,1,0:T(8,128)(2,1)S(1)} collective-permute-done((bf16[2,1,2,128,512]{4,3,2,1,0:T(8,128)(2,1)S(1)}, bf16[2,1,2,128,512]{4,3,2,1,0:T(8,128)(2,1)S(1)}, u32[]{:S(2)}, u32[]{:S(2)}) %collective-permute-start.5) | collective-permute-done | bytes 524320 | tf_op jit(solution)/shard_map/ppermute | solution.py:9
  362.4 10.9 %collective-permute-done.6 = bf16[2,1,2,128,512]{4,3,2,1,0:T(8,128)(2,1)S(1)} collective-permute-done((bf16[2,1,2,128,512]{4,3,2,1,0:T(8,128)(2,1)}, bf16[2,1,2,128,512]{4,3,2,1,0:T(8,128)(2,1)S(1)}, u32[]{:S(2)}, u32[]{:S(2)}) %collective-permute-start.6) | collective-permute-done | bytes 524320 | tf_op jit(solution)/shard_map/ppermute | solution.py:9
  375.9 23.1 %collective-permute-done.7 = f32[2,1,2,128,512]{4,3,2,1,0:T(8,128)S(1)} collective-permute-done((f32[2,1,2,128,512]{4,3,2,1,0:T(8,128)S(1)}, f32[2,1,2,128,512]{4,3,2,1,0:T(8,128)S(1)}, u32[]{:S(2)}, u32[]{:S(2)}) %collective-permute-start.7) | collective-permute-done | bytes 1048608 | tf_op jit(solution)/shard_map/ppermute | solution.py:9
  402.6 12.8 %collective-permute-done.8 = f32[2,1,2,128,512]{4,3,2,1,0:T(8,128)S(1)} collective-permute-done((f32[2,1,2,128,512]{4,3,2,1,0:T(8,128)S(1)}, f32[2,1,2,128,512]{4,3,2,1,0:T(8,128)S(1)}, u32[]{:S(2)}, u32[]{:S(2)}) %collective-permute-start.8) | collective-permute-done | bytes 1048608 | tf_op jit(solution)/shard_map/ppermute | solution.py:9
  421.1 12.8 %collective-permute-done.9 = f32[2,1,2,128,512]{4,3,2,1,0:T(8,128)S(1)} collective-permute-done((f32[2,1,2,128,512]{4,3,2,1,0:T(8,128)S(1)}, f32[2,1,2,128,512]{4,3,2,1,0:T(8,128)S(1)}, u32[]{:S(2)}, u32[]{:S(2)}) %collective-permute-start.9) | collective-permute-done | bytes 1048608 | tf_op jit(solution)/shard_map/ppermute | solution.py:9
  450.0 12.6 %collective-permute-done.10 = bf16[2,2,2,128,512]{4,3,1,2,0:T(8,128)(2,1)S(1)} collective-permute-done((bf16[2,2,2,128,512]{4,3,1,2,0:T(8,128)(2,1)S(1)}, bf16[2,2,2,128,512]{4,3,1,2,0:T(8,128)(2,1)S(1)}, u32[]{:S(2)}, u32[]{:S(2)}) %collective-permute-start.10) | collective-permute-done | bytes 1048608 | tf_op jit(solution)/shard_map/ppermute | solution.py:9
  466.6 12.4 %collective-permute-done.11 = bf16[2,2,2,128,512]{4,3,1,2,0:T(8,128)(2,1)S(1)} collective-permute-done((bf16[2,2,2,128,512]{4,3,1,2,0:T(8,128)(2,1)S(1)}, bf16[2,2,2,128,512]{4,3,1,2,0:T(8,128)(2,1)S(1)}, u32[]{:S(2)}, u32[]{:S(2)}) %collective-permute-start.11) | collective-permute-done | bytes 1048608 | tf_op jit(solution)/shard_map/ppermute | solution.py:9
  480.5 17.3 %collective-permute-start.12 = (bf16[2,2,2,128,512]{4,3,1,2,0:T(8,128)(2,1)S(1)}, bf16[2,2,2,128,512]{4,3,1,2,0:T(8,128)(2,1)S(1)}, u32[]{:S(2)}, u32[]{:S(2)}) collective-permute-start(bf16[2,2,2,128,512]{4,3,1,2,0:T(8,128)(2,1)S(1)} %get-tuple-element.8), channel_id=1, source_target_pairs={{0,64},{16,80},{32,96},{48,112},{64,0},{80,16},{96,32},{112,48},{1... | collective-permute-start | bytes 3145736 | tf_op jit(solution)/shard_map/ppermute | solution.py:9
  498.2 12.5 %collective-permute-done.12 = bf16[2,2,2,128,512]{4,3,1,2,0:T(8,128)(2,1)S(1)} collective-permute-done((bf16[2,2,2,128,512]{4,3,1,2,0:T(8,128)(2,1)S(1)}, bf16[2,2,2,128,512]{4,3,1,2,0:T(8,128)(2,1)S(1)}, u32[]{:S(2)}, u32[]{:S(2)}) %collective-permute-start.12) | collective-permute-done | bytes 1048608 | tf_op jit(solution)/shard_map/ppermute | solution.py:9
  514.1 5.8 collective-permute-done.13
  521.9 65.9 %all-gather.2.cloned.1.call-done = bf16[1024,1536]{0,1:T(8,128)(2,1)} async-done(((bf16[128,1536]{0,1:T(8,128)(2,1)}), bf16[1024,1536]{0,1:T(8,128)(2,1)}) %all-gather.2.cloned.1.call-update) | async-done | bytes 3145744 | tf_op jit(solution)/shard_map/all_gather | solution.py:176
  587.8 6.8 multiply_convert_fusion
  599.6 6.3 convolution_convert_fusion
  608.5 84.1 %all-reduce.5.cloned.1.call-done = (bf16[1024,3,512]{2,0,1:T(8,128)(2,1)}, bf16[128,512]{1,0:T(8,128)(2,1)}) async-done(((bf16[1024,3,512]{2,0,1:T(8,128)(2,1)}, bf16[128,512]{1,0:T(8,128)(2,1)}), (bf16[1024,3,512]{2,0,1:T(8,128)(2,1)}, bf16[128,512]{1,0:T(8,128)(2,1)})) %all-reduce.5.cloned.1.call-update) | async-done | bytes 3276816 | tf_op jit(solution)/shard_map/psum | solution.py:187
  694.3 35.9 %reduce-scatter.7.cloned.1.call-done = bf16[128,1024]{1,0:T(8,128)(2,1)} async-done(((bf16[1024,1024]{1,0:T(8,128)(2,1)}), bf16[128,1024]{1,0:T(8,128)(2,1)}) %reduce-scatter.7.cloned.1.call-update) | async-done | bytes 262160
  (171 shorter events, 119.0 us)
Async XLA Ops:
  11.3 36.5 %all-to-all-start = ((bf16[128,8,1024]{0,2,1:T(8,128)(2,1)}), bf16[128,8,1024]{0,2,1:T(8,128)(2,1)S(1)}, u32[]{:S(2)}, u32[]{:S(2)}) async-start(bf16[128,8,1024]{0,2,1:T(8,128)(2,1)} %bitcast.318), calls=%async_computation | async-start | bytes 4194304 | tf_op jit(solution)/shard_map/all_to_all | solution.py:127
  19.3 135.6 %reduce-scatter.5.cloned.1.call-start = ((), (), s32[]{:S(2)}) async-start(), calls=%async_computation.3 | async-start | bytes 7077888 | tf_op jit(solution)/shard_map/reduce_scatter | solution.py:129
  59.0 528.8 %all-gather.2.cloned.1.call-start = ((), (), s32[]{:S(2)}) async-start(), calls=%async_computation.4 | async-start | bytes 3538944 | tf_op jit(solution)/shard_map/all_gather | solution.py:176
  155.7 4.3 collective-permute-start
  162.6 49.0 %collective-permute-start.1 = (f32[2,2,2,128,512]{4,3,1,2,0:T(8,128)}, f32[2,2,2,128,512]{4,3,1,2,0:T(8,128)}, u32[]{:S(2)}, u32[]{:S(2)}) collective-permute-start(f32[2,2,2,128,512]{4,3,1,2,0:T(8,128)} %pad_maximum_fusion), channel_id=1, source_target_pairs={{0,64},{16,80},{32,96},{48,112},{64,0},{80,16},{96,32},{112,48},{1... | collective-permute-start | bytes 6291464 | tf_op jit(solution)/shard_map/ppermute | solution.py:9
  218.5 45.3 %collective-permute-start.2 = (f32[2,2,2,128,512]{4,3,1,2,0:T(8,128)}, f32[2,2,2,128,512]{4,3,1,2,0:T(8,128)}, u32[]{:S(2)}, u32[]{:S(2)}) collective-permute-start(f32[2,2,2,128,512]{4,3,1,2,0:T(8,128)} %maximum_select_fusion), channel_id=1, source_target_pairs={{0,32},{16,48},{32,0},{48,16},{64,96},{80,112},{96,64},{112,80},{1... | collective-permute-start | bytes 6291464 | tf_op jit(solution)/shard_map/ppermute | solution.py:9
  274.0 45.9 %collective-permute-start.3 = (f32[2,2,2,128,512]{4,3,1,2,0:T(8,128)}, f32[2,2,2,128,512]{4,3,1,2,0:T(8,128)S(1)}, u32[]{:S(2)}, u32[]{:S(2)}) collective-permute-start(f32[2,2,2,128,512]{4,3,1,2,0:T(8,128)} %maximum_select_fusion.1), channel_id=1, source_target_pairs={{0,16},{16,0},{32,48},{48,32},{64,80},{80,64},{96,112},{112,96},{1... | collective-permute-start | bytes 6291464 | tf_op jit(solution)/shard_map/ppermute | solution.py:9
  276.3 48.3 %copy-start.13 = (f32[2,128]{1,0:T(2,128)}, f32[2,128]{1,0:T(2,128)S(1)}, u32[]{:S(2)}) copy-start(f32[2,128]{1,0:T(2,128)S(1)} %get-tuple-element.80) | copy-start | bytes 3076
  276.3 48.3 %copy-start.15 = (f32[2,128]{1,0:T(2,128)}, f32[2,128]{1,0:T(2,128)S(1)}, u32[]{:S(2)}) copy-start(f32[2,128]{1,0:T(2,128)S(1)} %get-tuple-element.81) | copy-start | bytes 3076
  276.3 59.5 %copy-start.19 = (f32[2,128]{1,0:T(2,128)}, f32[2,128]{1,0:T(2,128)S(1)}, u32[]{:S(2)}) copy-start(f32[2,128]{1,0:T(2,128)S(1)} %get-tuple-element.78) | copy-start | bytes 3076
  276.3 59.5 %copy-start.21 = (f32[2,128]{1,0:T(2,128)}, f32[2,128]{1,0:T(2,128)S(1)}, u32[]{:S(2)}) copy-start(f32[2,128]{1,0:T(2,128)S(1)} %get-tuple-element.79) | copy-start | bytes 3076
  337.0 11.0 %collective-permute-start.4 = (bf16[2,1,2,128,512]{4,3,2,1,0:T(8,128)(2,1)S(1)}, bf16[2,1,2,128,512]{4,3,2,1,0:T(8,128)(2,1)S(1)}, u32[]{:S(2)}, u32[]{:S(2)}) collective-permute-start(bf16[2,1,2,128,512]{4,3,2,1,0:T(8,128)(2,1)S(1)} %fusion.32), channel_id=1, source_target_pairs={{0,16},{16,0},{32,48},{48,32},{64,80},{80,64},{96,112},{112,96},{1... | collective-permute-start | bytes 1572872 | tf_op jit(solution)/shard_map/ppermute | solution.py:9
  348.7 10.9 %collective-permute-start.5 = (bf16[2,1,2,128,512]{4,3,2,1,0:T(8,128)(2,1)S(1)}, bf16[2,1,2,128,512]{4,3,2,1,0:T(8,128)(2,1)S(1)}, u32[]{:S(2)}, u32[]{:S(2)}) collective-permute-start(bf16[2,1,2,128,512]{4,3,2,1,0:T(8,128)(2,1)S(1)} %get-tuple-element.17), channel_id=1, source_target_pairs={{0,32},{16,48},{32,0},{48,16},{64,96},{80,112},{96,64},{112,80},{1... | collective-permute-start | bytes 1572872 | tf_op jit(solution)/shard_map/ppermute | solution.py:9
  361.0 12.3 %collective-permute-start.6 = (bf16[2,1,2,128,512]{4,3,2,1,0:T(8,128)(2,1)}, bf16[2,1,2,128,512]{4,3,2,1,0:T(8,128)(2,1)S(1)}, u32[]{:S(2)}, u32[]{:S(2)}) collective-permute-start(bf16[2,1,2,128,512]{4,3,2,1,0:T(8,128)(2,1)} %get-tuple-element.15), channel_id=1, source_target_pairs={{0,64},{16,80},{32,96},{48,112},{64,0},{80,16},{96,32},{112,48},{1... | collective-permute-start | bytes 1572872 | tf_op jit(solution)/shard_map/ppermute | solution.py:9
  375.8 23.2 %collective-permute-start.7 = (f32[2,1,2,128,512]{4,3,2,1,0:T(8,128)S(1)}, f32[2,1,2,128,512]{4,3,2,1,0:T(8,128)S(1)}, u32[]{:S(2)}, u32[]{:S(2)}) collective-permute-start(f32[2,1,2,128,512]{4,3,2,1,0:T(8,128)S(1)} %pad_maximum_fusion.3), channel_id=1, source_target_pairs={{0,64},{16,80},{32,96},{48,112},{64,0},{80,16},{96,32},{112,48},{1... | collective-permute-start | bytes 3145736 | tf_op jit(solution)/shard_map/ppermute | solution.py:9
  399.7 15.6 %collective-permute-start.8 = (f32[2,1,2,128,512]{4,3,2,1,0:T(8,128)S(1)}, f32[2,1,2,128,512]{4,3,2,1,0:T(8,128)S(1)}, u32[]{:S(2)}, u32[]{:S(2)}) collective-permute-start(f32[2,1,2,128,512]{4,3,2,1,0:T(8,128)S(1)} %maximum_select_fusion.3), channel_id=1, source_target_pairs={{0,32},{16,48},{32,0},{48,16},{64,96},{80,112},{96,64},{112,80},{1... | collective-permute-start | bytes 3145736 | tf_op jit(solution)/shard_map/ppermute | solution.py:9
  416.7 17.2 %collective-permute-start.9 = (f32[2,1,2,128,512]{4,3,2,1,0:T(8,128)S(1)}, f32[2,1,2,128,512]{4,3,2,1,0:T(8,128)S(1)}, u32[]{:S(2)}, u32[]{:S(2)}) collective-permute-start(f32[2,1,2,128,512]{4,3,2,1,0:T(8,128)S(1)} %maximum_select_fusion.4), channel_id=1, source_target_pairs={{0,16},{16,0},{32,48},{48,32},{64,80},{80,64},{96,112},{112,96},{1... | collective-permute-start | bytes 3145736 | tf_op jit(solution)/shard_map/ppermute | solution.py:9
  446.0 16.6 %collective-permute-start.10 = (bf16[2,2,2,128,512]{4,3,1,2,0:T(8,128)(2,1)S(1)}, bf16[2,2,2,128,512]{4,3,1,2,0:T(8,128)(2,1)S(1)}, u32[]{:S(2)}, u32[]{:S(2)}) collective-permute-start(bf16[2,2,2,128,512]{4,3,1,2,0:T(8,128)(2,1)S(1)} %fusion.3), channel_id=1, source_target_pairs={{0,16},{16,0},{32,48},{48,32},{64,80},{80,64},{96,112},{112,96},{1... | collective-permute-start | bytes 3145736 | tf_op jit(solution)/shard_map/ppermute | solution.py:9
  464.1 14.9 %collective-permute-start.11 = (bf16[2,2,2,128,512]{4,3,1,2,0:T(8,128)(2,1)S(1)}, bf16[2,2,2,128,512]{4,3,1,2,0:T(8,128)(2,1)S(1)}, u32[]{:S(2)}, u32[]{:S(2)}) collective-permute-start(bf16[2,2,2,128,512]{4,3,1,2,0:T(8,128)(2,1)S(1)} %get-tuple-element.10), channel_id=1, source_target_pairs={{0,32},{16,48},{32,0},{48,16},{64,96},{80,112},{96,64},{112,80},{1... | collective-permute-start | bytes 3145736 | tf_op jit(solution)/shard_map/ppermute | solution.py:9
  480.5 30.1 %collective-permute-start.12 = (bf16[2,2,2,128,512]{4,3,1,2,0:T(8,128)(2,1)S(1)}, bf16[2,2,2,128,512]{4,3,1,2,0:T(8,128)(2,1)S(1)}, u32[]{:S(2)}, u32[]{:S(2)}) collective-permute-start(bf16[2,2,2,128,512]{4,3,1,2,0:T(8,128)(2,1)S(1)} %get-tuple-element.8), channel_id=1, source_target_pairs={{0,64},{16,80},{32,96},{48,112},{64,0},{80,16},{96,32},{112,48},{1... | collective-permute-start | bytes 3145736 | tf_op jit(solution)/shard_map/ppermute | solution.py:9
  512.8 7.1 collective-permute-start.13
  519.9 67.8 %copy-start.8 = (bf16[8,128,1024]{2,1,0:T(8,128)(2,1)S(1)}, bf16[8,128,1024]{2,1,0:T(8,128)(2,1)}, u32[]{:S(2)}) copy-start(bf16[8,128,1024]{2,1,0:T(8,128)(2,1)} %copy.91) | copy-start | bytes 6291460
  521.2 171.4 %all-reduce.5.cloned.1.call-start = ((), (), s32[]{:S(2)}) async-start(), calls=%async_computation.6 | async-start | bytes 6553600 | tf_op jit(solution)/shard_map/psum | solution.py:187
  599.3 130.9 %reduce-scatter.7.cloned.1.call-start = ((), (), s32[]{:S(2)}) async-start(), calls=%async_computation.5 | async-start | bytes 2359296
  (18 other events, 40.3 us)
Sparse Core Ops, SparseCore 0:
  59.1 95.7 reduce-scatter.4
  521.3 66.4 all-gather.1
  599.4 93.1 all-reduce.4
  695.6 34.5 reduce-scatter.6
where the time goes:
time: 751 us; the launch traced here: 742 us
  waiting for transfers between devices  556 us (74%)
  starting transfers between devices  56.6 us (8%)
  matrix products  43.9 us (6%)
  other arithmetic  39.1 us (5%)
  local copies, waits for them, and re-layouts  31.3 us (4%)
  between operations  15.8 us (2%)
    ppermute x12, waiting for transfers between devices, partner_2(): lax.ppermute(shard, axis, [(i, i ^ 1 << stride) for i in range(lax.axis_s...  245 us
    reduce_scatter x1, waiting for transfers between devices, local(): lax.psum_scatter(jnp.dot(spread, flat_weight, preferred_element_type=jnp....  95.1 us
    psum x1, waiting for transfers between devices, local(): lax.psum((weight_total * grad_scale).astype(jnp.bfloat16), 'dp')  84.1 us
    all_gather x1, waiting for transfers between devices, local(): shard_rows = lax.all_gather(d_projected, 'seq', axis=0, tiled=True)  65.9 us
    ppermute x12, starting transfers between devices, partner_2(): lax.ppermute(shard, axis, [(i, i ^ 1 << stride) for i in range(lax.axis_s...  44.5 us
    unnamed x5, waiting for transfers between devices  36 us
    all_to_all x1, waiting for transfers between devices, local(): lax.all_to_all(tokens[0], 'seq', split_axis=1, concat_axis=0, tiled=True)  23.8 us
    unnamed x53, local copies, waits for them, and re-layouts  20 us
  transfers between devices with their start and end apart: 19, of which 18 were waited for; matrix products, arithmetic and copies ran while one was open for 3% of the time, Pallas kernels for 0%

commit v1 on v0

--- a/solution.py
+++ b/solution.py
@@ -173,7 +173,9 @@
             d_projected + short_taps[:, tap_pos, :] * ext_next[tap_pos : tap_pos + tok_rows]
         )
     d_projected = d_projected.astype(jnp.bfloat16).reshape(tok_rows, 3 * chan_cols)
-    shard_rows = lax.all_gather(d_projected, "seq", axis=0, tiled=True)
+    shard_rows = jnp.concatenate(
+        lax.all_to_all(jnp.stack([d_projected] * lax.axis_size("seq")), "seq", 0, 0), axis=0
+    )
     weight_total = lax.dot_general(
         spread, shard_rows, (((0,), (0,)), ((), ())), preferred_element_type=jnp.float32
     )

time: 751 us -> 719 us (0.957)
  waiting for transfers between devices: 556 us -> 513 us
  starting transfers between devices: 56.6 us -> 64.5 us
    all_gather x1 -> x0, waiting for transfers between devices: 65.9 us -> none  [local(): shard_rows = lax.all_gather(d_projected, 'seq', axis=0, tiled=True)]
    all_to_all x0 -> x1, waiting for transfers between devices: none -> 24.1 us  [local(): lax.all_to_all(jnp.stack([d_projected] * lax.axis_size('seq')), 'seq', 0, 0)]
    all_to_all x0 -> x1, starting transfers between devices: none -> 8.4 us  [local(): lax.all_to_all(jnp.stack([d_projected] * lax.axis_size('seq')), 'seq', 0, 0)]
    unnamed x53 -> x55, local copies, waits for them, and re-layouts: 20 us -> 17.6 us
    unnamed x5 -> x4, waiting for transfers between devices: 36 us -> 36.1 us
where the time goes in v1:
time: 719 us; the launch traced here: 710 us
  waiting for transfers between devices  513 us (71%)
  starting transfers between devices  64.5 us (9%)
  matrix products  43 us (6%)
  other arithmetic  40.8 us (6%)
  local copies, waits for them, and re-layouts  33.2 us (5%)
  between operations  15.8 us (2%)
    ppermute x12, waiting for transfers between devices, partner_2(): lax.ppermute(shard, axis, [(i, i ^ 1 << stride) for i in range(lax.axis_s...  245 us
    reduce_scatter x1, waiting for transfers between devices, local(): lax.psum_scatter(jnp.dot(spread, flat_weight, preferred_element_type=jnp....  95.1 us
    psum x1, waiting for transfers between devices, local(): lax.psum((weight_total * grad_scale).astype(jnp.bfloat16), 'dp')  81.2 us
    ppermute x12, starting transfers between devices, partner_2(): lax.ppermute(shard, axis, [(i, i ^ 1 << stride) for i in range(lax.axis_s...  43.7 us
    unnamed x4, waiting for transfers between devices  36.1 us
    all_to_all x1, waiting for transfers between devices, local(): lax.all_to_all(tokens[0], 'seq', split_axis=1, concat_axis=0, tiled=True)  25.5 us
    all_to_all x1, waiting for transfers between devices, local(): lax.all_to_all(jnp.stack([d_projected] * lax.axis_size('seq')), 'seq', 0, 0)  24.1 us
    unnamed x55, local copies, waits for them, and re-layouts  17.6 us
  transfers between devices with their start and end apart: 19, of which 18 were waited for; matrix products, arithmetic and copies ran while one was open for 3% of the time, Pallas kernels for 0%

profile of v1, /device:TPU:0, one launch (start us, length us, event | category | flops | bytes accessed | tf_op | source)
XLA Modules:
  0.0 710.4 jit_solution(11297315026671153554)
XLA Ops:
  13.1 8.3 %all-to-all-start = ((bf16[128,8,1024]{2,0,1:T(8,128)(2,1)}), bf16[128,8,1024]{2,0,1:T(8,128)(2,1)}, u32[]{:S(2)}, u32[]{:S(2)}) async-start(bf16[128,8,1024]{2,0,1:T(8,128)(2,1)} %copy.65), calls=%async_computation | async-start | bytes 4194304 | tf_op jit(solution)/shard_map/all_to_all | solution.py:127
  24.5 25.5 %all-to-all-done = bf16[128,8,1024]{2,0,1:T(8,128)(2,1)} async-done(((bf16[128,8,1024]{2,0,1:T(8,128)(2,1)}), bf16[128,8,1024]{2,0,1:T(8,128)(2,1)}, u32[]{:S(2)}, u32[]{:S(2)}) %all-to-all-start) | async-done | bytes 2097184 | tf_op jit(solution)/shard_map/all_to_all | solution.py:127
  50.0 8.6 %fusion.206 = f32[1024,1536]{1,0:T(8,128)} fusion(bf16[1024,1024]{1,0:T(8,128)(2,1)} %bitcast.2, bf16[1024,1536]{0,1:T(8,128)(2,1)} %bitcast.329), kind=kOutput, calls=%fused_computation.318 | convolution fusion | flops 3221225472 | bytes 11534336 | tf_op jit(solution)/shard_map/dot_general | solution.py:130
  59.3 95.1 %reduce-scatter.5.cloned.1.call-done = f32[128,1536]{1,0:T(8,128)} async-done(((f32[1024,1536]{1,0:T(8,128)}), f32[128,1536]{1,0:T(8,128)}) %reduce-scatter.5.cloned.1.call-update) | async-done | bytes 786448 | tf_op jit(solution)/shard_map/reduce_scatter | solution.py:129
  167.2 44.0 %collective-permute-done.1 = f32[2,2,2,128,512]{4,3,1,2,0:T(8,128)} collective-permute-done((f32[2,2,2,128,512]{4,3,1,2,0:T(8,128)}, f32[2,2,2,128,512]{4,3,1,2,0:T(8,128)}, u32[]{:S(2)}, u32[]{:S(2)}) %collective-permute-start.1) | collective-permute-done | bytes 2097184 | tf_op jit(solution)/shard_map/ppermute | solution.py:9
  220.3 43.1 %collective-permute-done.2 = f32[2,2,2,128,512]{4,3,1,2,0:T(8,128)} collective-permute-done((f32[2,2,2,128,512]{4,3,1,2,0:T(8,128)}, f32[2,2,2,128,512]{4,3,1,2,0:T(8,128)}, u32[]{:S(2)}, u32[]{:S(2)}) %collective-permute-start.2) | collective-permute-done | bytes 2097184 | tf_op jit(solution)/shard_map/ppermute | solution.py:9
  275.9 43.6 %collective-permute-done.3 = f32[2,2,2,128,512]{4,3,1,2,0:T(8,128)S(1)} collective-permute-done((f32[2,2,2,128,512]{4,3,1,2,0:T(8,128)}, f32[2,2,2,128,512]{4,3,1,2,0:T(8,128)S(1)}, u32[]{:S(2)}, u32[]{:S(2)}) %collective-permute-start.3) | collective-permute-done | bytes 2097184 | tf_op jit(solution)/shard_map/ppermute | solution.py:9
  338.8 8.7 %collective-permute-done.4 = bf16[2,1,2,128,512]{4,3,2,1,0:T(8,128)(2,1)S(1)} collective-permute-done((bf16[2,1,2,128,512]{4,3,2,1,0:T(8,128)(2,1)S(1)}, bf16[2,1,2,128,512]{4,3,2,1,0:T(8,128)(2,1)S(1)}, u32[]{:S(2)}, u32[]{:S(2)}) %collective-permute-start.4) | collective-permute-done | bytes 524320 | tf_op jit(solution)/shard_map/ppermute | solution.py:9
  351.0 9.0 %collective-permute-done.5 = bf16[2,1,2,128,512]{4,3,2,1,0:T(8,128)(2,1)S(1)} collective-permute-done((bf16[2,1,2,128,512]{4,3,2,1,0:T(8,128)(2,1)}, bf16[2,1,2,128,512]{4,3,2,1,0:T(8,128)(2,1)S(1)}, u32[]{:S(2)}, u32[]{:S(2)}) %collective-permute-start.5) | collective-permute-done | bytes 524320 | tf_op jit(solution)/shard_map/ppermute | solution.py:9
  362.9 10.9 %collective-permute-done.6 = bf16[2,1,2,128,512]{4,3,2,1,0:T(8,128)(2,1)S(1)} collective-permute-done((bf16[2,1,2,128,512]{4,3,2,1,0:T(8,128)(2,1)}, bf16[2,1,2,128,512]{4,3,2,1,0:T(8,128)(2,1)S(1)}, u32[]{:S(2)}, u32[]{:S(2)}) %collective-permute-start.6) | collective-permute-done | bytes 524320 | tf_op jit(solution)/shard_map/ppermute | solution.py:9
  376.4 23.1 %collective-permute-done.7 = f32[2,1,2,128,512]{4,3,2,1,0:T(8,128)S(1)} collective-permute-done((f32[2,1,2,128,512]{4,3,2,1,0:T(8,128)S(1)}, f32[2,1,2,128,512]{4,3,2,1,0:T(8,128)S(1)}, u32[]{:S(2)}, u32[]{:S(2)}) %collective-permute-start.7) | collective-permute-done | bytes 1048608 | tf_op jit(solution)/shard_map/ppermute | solution.py:9
  403.1 12.8 %collective-permute-done.8 = f32[2,1,2,128,512]{4,3,2,1,0:T(8,128)S(1)} collective-permute-done((f32[2,1,2,128,512]{4,3,2,1,0:T(8,128)S(1)}, f32[2,1,2,128,512]{4,3,2,1,0:T(8,128)S(1)}, u32[]{:S(2)}, u32[]{:S(2)}) %collective-permute-start.8) | collective-permute-done | bytes 1048608 | tf_op jit(solution)/shard_map/ppermute | solution.py:9
  422.1 12.8 %collective-permute-done.9 = f32[2,1,2,128,512]{4,3,2,1,0:T(8,128)S(1)} collective-permute-done((f32[2,1,2,128,512]{4,3,2,1,0:T(8,128)S(1)}, f32[2,1,2,128,512]{4,3,2,1,0:T(8,128)S(1)}, u32[]{:S(2)}, u32[]{:S(2)}) %collective-permute-start.9) | collective-permute-done | bytes 1048608 | tf_op jit(solution)/shard_map/ppermute | solution.py:9
  451.0 12.6 %collective-permute-done.10 = bf16[2,2,2,128,512]{4,3,1,2,0:T(8,128)(2,1)S(1)} collective-permute-done((bf16[2,2,2,128,512]{4,3,1,2,0:T(8,128)(2,1)S(1)}, bf16[2,2,2,128,512]{4,3,1,2,0:T(8,128)(2,1)S(1)}, u32[]{:S(2)}, u32[]{:S(2)}) %collective-permute-start.10) | collective-permute-done | bytes 1048608 | tf_op jit(solution)/shard_map/ppermute | solution.py:9
  467.6 12.4 %collective-permute-done.11 = bf16[2,2,2,128,512]{4,3,1,2,0:T(8,128)(2,1)S(1)} collective-permute-done((bf16[2,2,2,128,512]{4,3,1,2,0:T(8,128)(2,1)S(1)}, bf16[2,2,2,128,512]{4,3,1,2,0:T(8,128)(2,1)S(1)}, u32[]{:S(2)}, u32[]{:S(2)}) %collective-permute-start.11) | collective-permute-done | bytes 1048608 | tf_op jit(solution)/shard_map/ppermute | solution.py:9
  481.6 16.1 %collective-permute-start.12 = (bf16[2,2,2,128,512]{4,3,1,2,0:T(8,128)(2,1)S(1)}, bf16[2,2,2,128,512]{4,3,1,2,0:T(8,128)(2,1)S(1)}, u32[]{:S(2)}, u32[]{:S(2)}) collective-permute-start(bf16[2,2,2,128,512]{4,3,1,2,0:T(8,128)(2,1)S(1)} %get-tuple-element.8), channel_id=1, source_target_pairs={{0,64},{16,80},{32,96},{48,112},{64,0},{80,16},{96,32},{112,48},{1... | collective-permute-start | bytes 3145736 | tf_op jit(solution)/shard_map/ppermute | solution.py:9
  498.0 12.5 %collective-permute-done.12 = bf16[2,2,2,128,512]{4,3,1,2,0:T(8,128)(2,1)S(1)} collective-permute-done((bf16[2,2,2,128,512]{4,3,1,2,0:T(8,128)(2,1)S(1)}, bf16[2,2,2,128,512]{4,3,1,2,0:T(8,128)(2,1)S(1)}, u32[]{:S(2)}, u32[]{:S(2)}) %collective-permute-start.12) | collective-permute-done | bytes 1048608 | tf_op jit(solution)/shard_map/ppermute | solution.py:9
  513.9 5.8 collective-permute-done.13
  522.3 8.4 %all-to-all-start.1 = ((bf16[8,128,1536]{1,2,0:T(8,128)(2,1)}), bf16[8,128,1536]{1,2,0:T(8,128)(2,1)S(1)}, u32[]{:S(2)}, u32[]{:S(2)}) async-start(bf16[8,128,1536]{1,2,0:T(8,128)(2,1)} %stack.271), calls=%async_computation.2 | async-start | bytes 6291456 | tf_op jit(solution)/shard_map/all_to_all | solution.py:177
  532.4 24.1 %all-to-all-done.1 = bf16[8,128,1536]{1,2,0:T(8,128)(2,1)S(1)} async-done(((bf16[8,128,1536]{1,2,0:T(8,128)(2,1)}), bf16[8,128,1536]{1,2,0:T(8,128)(2,1)S(1)}, u32[]{:S(2)}, u32[]{:S(2)}) %all-to-all-start.1) | async-done | bytes 3145760 | tf_op jit(solution)/shard_map/all_to_all | solution.py:177
  556.4 6.0 fusion
  570.3 6.3 convolution_convert_fusion
  579.2 81.2 %all-reduce.5.cloned.1.call-done = (bf16[1024,3,512]{2,0,1:T(8,128)(2,1)}, bf16[128,512]{1,0:T(8,128)(2,1)}) async-done(((bf16[1024,3,512]{2,0,1:T(8,128)(2,1)}, bf16[128,512]{1,0:T(8,128)(2,1)}), (bf16[1024,3,512]{2,0,1:T(8,128)(2,1)}, bf16[128,512]{1,0:T(8,128)(2,1)})) %all-reduce.5.cloned.1.call-update) | async-done | bytes 3276816 | tf_op jit(solution)/shard_map/psum | solution.py:189
  662.0 36.0 %reduce-scatter.7.cloned.1.call-done = bf16[128,1024]{1,0:T(8,128)(2,1)} async-done(((bf16[1024,1024]{1,0:T(8,128)(2,1)}), bf16[128,1024]{1,0:T(8,128)(2,1)}) %reduce-scatter.7.cloned.1.call-update) | async-done | bytes 262160
  (174 shorter events, 127.9 us)
Async XLA Ops:
  13.1 8.3 %copy-start.8 = (bf16[1024,3,512]{2,0,1:T(8,128)(2,1)S(1)}, bf16[1024,3,512]{2,0,1:T(8,128)(2,1)}, u32[]{:S(2)}) copy-start(bf16[1024,3,512]{2,0,1:T(8,128)(2,1)} %param.7) | copy-start | bytes 9437188
  13.1 36.9 %all-to-all-start = ((bf16[128,8,1024]{2,0,1:T(8,128)(2,1)}), bf16[128,8,1024]{2,0,1:T(8,128)(2,1)}, u32[]{:S(2)}, u32[]{:S(2)}) async-start(bf16[128,8,1024]{2,0,1:T(8,128)(2,1)} %copy.65), calls=%async_computation | async-start | bytes 4194304 | tf_op jit(solution)/shard_map/all_to_all | solution.py:127
  21.4 133.1 %reduce-scatter.5.cloned.1.call-start = ((), (), s32[]{:S(2)}) async-start(), calls=%async_computation.4 | async-start | bytes 7077888 | tf_op jit(solution)/shard_map/reduce_scatter | solution.py:129
  155.3 4.3 collective-permute-start
  162.2 49.0 %collective-permute-start.1 = (f32[2,2,2,128,512]{4,3,1,2,0:T(8,128)}, f32[2,2,2,128,512]{4,3,1,2,0:T(8,128)}, u32[]{:S(2)}, u32[]{:S(2)}) collective-permute-start(f32[2,2,2,128,512]{4,3,1,2,0:T(8,128)} %pad_maximum_fusion), channel_id=1, source_target_pairs={{0,64},{16,80},{32,96},{48,112},{64,0},{80,16},{96,32},{112,48},{1... | collective-permute-start | bytes 6291464 | tf_op jit(solution)/shard_map/ppermute | solution.py:9
  218.1 45.3 %collective-permute-start.2 = (f32[2,2,2,128,512]{4,3,1,2,0:T(8,128)}, f32[2,2,2,128,512]{4,3,1,2,0:T(8,128)}, u32[]{:S(2)}, u32[]{:S(2)}) collective-permute-start(f32[2,2,2,128,512]{4,3,1,2,0:T(8,128)} %maximum_select_fusion), channel_id=1, source_target_pairs={{0,32},{16,48},{32,0},{48,16},{64,96},{80,112},{96,64},{112,80},{1... | collective-permute-start | bytes 6291464 | tf_op jit(solution)/shard_map/ppermute | solution.py:9
  273.6 45.9 %collective-permute-start.3 = (f32[2,2,2,128,512]{4,3,1,2,0:T(8,128)}, f32[2,2,2,128,512]{4,3,1,2,0:T(8,128)S(1)}, u32[]{:S(2)}, u32[]{:S(2)}) collective-permute-start(f32[2,2,2,128,512]{4,3,1,2,0:T(8,128)} %maximum_select_fusion.1), channel_id=1, source_target_pairs={{0,16},{16,0},{32,48},{48,32},{64,80},{80,64},{96,112},{112,96},{1... | collective-permute-start | bytes 6291464 | tf_op jit(solution)/shard_map/ppermute | solution.py:9
  275.9 48.3 %copy-start.14 = (f32[2,128]{1,0:T(2,128)}, f32[2,128]{1,0:T(2,128)S(1)}, u32[]{:S(2)}) copy-start(f32[2,128]{1,0:T(2,128)S(1)} %get-tuple-element.80) | copy-start | bytes 3076
  275.9 48.3 %copy-start.16 = (f32[2,128]{1,0:T(2,128)}, f32[2,128]{1,0:T(2,128)S(1)}, u32[]{:S(2)}) copy-start(f32[2,128]{1,0:T(2,128)S(1)} %get-tuple-element.81) | copy-start | bytes 3076
  275.9 59.5 %copy-start.20 = (f32[2,128]{1,0:T(2,128)}, f32[2,128]{1,0:T(2,128)S(1)}, u32[]{:S(2)}) copy-start(f32[2,128]{1,0:T(2,128)S(1)} %get-tuple-element.78) | copy-start | bytes 3076
  275.9 59.5 %copy-start.22 = (f32[2,128]{1,0:T(2,128)}, f32[2,128]{1,0:T(2,128)S(1)}, u32[]{:S(2)}) copy-start(f32[2,128]{1,0:T(2,128)S(1)} %get-tuple-element.79) | copy-start | bytes 3076
  336.6 11.0 %collective-permute-start.4 = (bf16[2,1,2,128,512]{4,3,2,1,0:T(8,128)(2,1)S(1)}, bf16[2,1,2,128,512]{4,3,2,1,0:T(8,128)(2,1)S(1)}, u32[]{:S(2)}, u32[]{:S(2)}) collective-permute-start(bf16[2,1,2,128,512]{4,3,2,1,0:T(8,128)(2,1)S(1)} %fusion.34), channel_id=1, source_target_pairs={{0,16},{16,0},{32,48},{48,32},{64,80},{80,64},{96,112},{112,96},{1... | collective-permute-start | bytes 1572872 | tf_op jit(solution)/shard_map/ppermute | solution.py:9
  349.0 11.0 %collective-permute-start.5 = (bf16[2,1,2,128,512]{4,3,2,1,0:T(8,128)(2,1)}, bf16[2,1,2,128,512]{4,3,2,1,0:T(8,128)(2,1)S(1)}, u32[]{:S(2)}, u32[]{:S(2)}) collective-permute-start(bf16[2,1,2,128,512]{4,3,2,1,0:T(8,128)(2,1)} %get-tuple-element.17), channel_id=1, source_target_pairs={{0,32},{16,48},{32,0},{48,16},{64,96},{80,112},{96,64},{112,80},{1... | collective-permute-start | bytes 1572872 | tf_op jit(solution)/shard_map/ppermute | solution.py:9
  361.5 12.3 %collective-permute-start.6 = (bf16[2,1,2,128,512]{4,3,2,1,0:T(8,128)(2,1)}, bf16[2,1,2,128,512]{4,3,2,1,0:T(8,128)(2,1)S(1)}, u32[]{:S(2)}, u32[]{:S(2)}) collective-permute-start(bf16[2,1,2,128,512]{4,3,2,1,0:T(8,128)(2,1)} %get-tuple-element.15), channel_id=1, source_target_pairs={{0,64},{16,80},{32,96},{48,112},{64,0},{80,16},{96,32},{112,48},{1... | collective-permute-start | bytes 1572872 | tf_op jit(solution)/shard_map/ppermute | solution.py:9
  376.3 23.2 %collective-permute-start.7 = (f32[2,1,2,128,512]{4,3,2,1,0:T(8,128)S(1)}, f32[2,1,2,128,512]{4,3,2,1,0:T(8,128)S(1)}, u32[]{:S(2)}, u32[]{:S(2)}) collective-permute-start(f32[2,1,2,128,512]{4,3,2,1,0:T(8,128)S(1)} %pad_maximum_fusion.3), channel_id=1, source_target_pairs={{0,64},{16,80},{32,96},{48,112},{64,0},{80,16},{96,32},{112,48},{1... | collective-permute-start | bytes 3145736 | tf_op jit(solution)/shard_map/ppermute | solution.py:9
  400.2 15.6 %collective-permute-start.8 = (f32[2,1,2,128,512]{4,3,2,1,0:T(8,128)S(1)}, f32[2,1,2,128,512]{4,3,2,1,0:T(8,128)S(1)}, u32[]{:S(2)}, u32[]{:S(2)}) collective-permute-start(f32[2,1,2,128,512]{4,3,2,1,0:T(8,128)S(1)} %maximum_select_fusion.3), channel_id=1, source_target_pairs={{0,32},{16,48},{32,0},{48,16},{64,96},{80,112},{96,64},{112,80},{1... | collective-permute-start | bytes 3145736 | tf_op jit(solution)/shard_map/ppermute | solution.py:9
  417.2 17.7 %collective-permute-start.9 = (f32[2,1,2,128,512]{4,3,2,1,0:T(8,128)S(1)}, f32[2,1,2,128,512]{4,3,2,1,0:T(8,128)S(1)}, u32[]{:S(2)}, u32[]{:S(2)}) collective-permute-start(f32[2,1,2,128,512]{4,3,2,1,0:T(8,128)S(1)} %maximum_select_fusion.4), channel_id=1, source_target_pairs={{0,16},{16,0},{32,48},{48,32},{64,80},{80,64},{96,112},{112,96},{1... | collective-permute-start | bytes 3145736 | tf_op jit(solution)/shard_map/ppermute | solution.py:9
  447.0 16.6 %collective-permute-start.10 = (bf16[2,2,2,128,512]{4,3,1,2,0:T(8,128)(2,1)S(1)}, bf16[2,2,2,128,512]{4,3,1,2,0:T(8,128)(2,1)S(1)}, u32[]{:S(2)}, u32[]{:S(2)}) collective-permute-start(bf16[2,2,2,128,512]{4,3,1,2,0:T(8,128)(2,1)S(1)} %fusion.5), channel_id=1, source_target_pairs={{0,16},{16,0},{32,48},{48,32},{64,80},{80,64},{96,112},{112,96},{1... | collective-permute-start | bytes 3145736 | tf_op jit(solution)/shard_map/ppermute | solution.py:9
  465.1 14.9 %collective-permute-start.11 = (bf16[2,2,2,128,512]{4,3,1,2,0:T(8,128)(2,1)S(1)}, bf16[2,2,2,128,512]{4,3,1,2,0:T(8,128)(2,1)S(1)}, u32[]{:S(2)}, u32[]{:S(2)}) collective-permute-start(bf16[2,2,2,128,512]{4,3,1,2,0:T(8,128)(2,1)S(1)} %get-tuple-element.10), channel_id=1, source_target_pairs={{0,32},{16,48},{32,0},{48,16},{64,96},{80,112},{96,64},{112,80},{1... | collective-permute-start | bytes 3145736 | tf_op jit(solution)/shard_map/ppermute | solution.py:9
  481.6 28.9 %collective-permute-start.12 = (bf16[2,2,2,128,512]{4,3,1,2,0:T(8,128)(2,1)S(1)}, bf16[2,2,2,128,512]{4,3,1,2,0:T(8,128)(2,1)S(1)}, u32[]{:S(2)}, u32[]{:S(2)}) collective-permute-start(bf16[2,2,2,128,512]{4,3,1,2,0:T(8,128)(2,1)S(1)} %get-tuple-element.8), channel_id=1, source_target_pairs={{0,64},{16,80},{32,96},{48,112},{64,0},{80,16},{96,32},{112,48},{1... | collective-permute-start | bytes 3145736 | tf_op jit(solution)/shard_map/ppermute | solution.py:9
  512.6 7.1 collective-permute-start.13
  522.3 34.1 %all-to-all-start.1 = ((bf16[8,128,1536]{1,2,0:T(8,128)(2,1)}), bf16[8,128,1536]{1,2,0:T(8,128)(2,1)S(1)}, u32[]{:S(2)}, u32[]{:S(2)}) async-start(bf16[8,128,1536]{1,2,0:T(8,128)(2,1)} %stack.271), calls=%async_computation.2 | async-start | bytes 6291456 | tf_op jit(solution)/shard_map/all_to_all | solution.py:177
  530.7 129.7 %all-reduce.5.cloned.1.call-start = ((), (), s32[]{:S(2)}) async-start(), calls=%async_computation.6 | async-start | bytes 6553600 | tf_op jit(solution)/shard_map/psum | solution.py:189
  567.2 130.9 %reduce-scatter.7.cloned.1.call-start = ((), (), s32[]{:S(2)}) async-start(), calls=%async_computation.5 | async-start | bytes 2359296
  (19 other events, 41.8 us)
Sparse Core Ops, SparseCore 0:
  58.7 95.7 reduce-scatter.4
  567.3 93.0 all-reduce.4
  663.5 34.5 reduce-scatter.6
